TPU v7x, 32 devices: a whole 2x2x4 slice. The times are simulated.
32 devices in a mesh: clip: 2 (over y), frame: 4 (over z), track: 4 (over x, core).
Axes of the slice: x: 2, y: 2, z: 4, core: 2. Of those that a mesh axis runs over, the one named last changes fastest.
Arguments:
- feature_maps: bfloat16 [8, 4096, 256], P(('clip', 'frame')), parts along dimension 0, may hold values from -6 to 6
- query_frame: int32 [1024], P('clip'), parts along dimension 0, may hold values from 0 to 3
- query_row: int32 [1024], P('clip'), parts along dimension 0, may hold values from 0 to 63
- query_col: int32 [1024], P('clip'), parts along dimension 0, may hold values from 0 to 63
- track_order: int32 [1024], P('clip'), parts along dimension 0, may hold values from 0 to 511, each once
- conv_weight: float32 [16, 9], replicated, may hold values from -2 to 2
- conv_bias: float32 [16], replicated, may hold values from -2 to 2
- head_weight: float32 [16], replicated, may hold values from -2 to 2
- mix_in: bfloat16 [256, 1024], replicated, may hold values from -0.375 to 0.375
- temporal_taps: float32 [3, 1024], replicated, may hold values from -2.5 to 2.5
- mix_gain: float32 [1024], replicated, may hold values from 0.25 to 1.75
- mix_out: bfloat16 [1024, 3], replicated, may hold values from -0.1875 to 0.1875
Outputs:
- estimates: float32 [1024, 3, 4], P(('clip', 'frame', 'track')), parts along dimension 0
There are 2 independent parts, one for each index of `clip`. A program takes and returns all parts, laid end to end along the dimension named above; an argument that names none is the same for every part. Nothing has to cross between parts.
Inputs may be any that keep to these rules, and one draw needn't show every extreme that they name: `track_order`: each track appears in exactly one slot.
All inputs are finite; a program needn't handle non-finite values.
Results may differ from a plain program's by a relative error of at most 0.0053.
Values may be sent and summed in bfloat16 or wider, within the bound.
No kernel may reach another device: no remote copies, remote signals or barrier semaphores. Data moves between devices by JAX's collectives and lax.ppermute only.
A program may use at most 64 MiB of HBM per device.

v0:
```python
import math
import jax
import jax.numpy as jnp
from jax import lax
from jax.sharding import PartitionSpec as P

GRID_H = 64
GRID_W = 64


def padded_2(block, sides, width):
    for axis, dim in sides:
        count = lax.axis_size(axis)
        forward = [(i, i + 1) for i in range(count - 1)]
        backward = [(target, source) for source, target in forward]
        low = lax.ppermute(
            lax.slice_in_dim(block, block.shape[dim] - width, None, axis=dim), axis, forward
        )
        high = lax.ppermute(lax.slice_in_dim(block, 0, width, axis=dim), axis, backward)
        block = jnp.concatenate([low, block, high], axis=dim)
    return block


def conv_logits(cost, conv_weight, conv_bias, head_weight):
    height, width = (cost.shape[1], cost.shape[2])
    padded = jnp.pad(cost, ((0, 0), (1, 1), (1, 1)))
    logit = jnp.zeros(cost.shape, jnp.float32)
    for channel in range(conv_weight.shape[0]):
        acc = jnp.zeros(cost.shape, jnp.float32) + conv_bias[channel]
        for tap in range(9):
            acc = (
                acc
                + conv_weight[channel, tap]
                * padded[:, tap // 3 : tap // 3 + height, tap % 3 : tap % 3 + width]
            )
        logit = logit + head_weight[channel] * jax.nn.relu(acc)
    return logit


def block_terms(qblock, maps, conv_weight, conv_bias, head_weight, row_pos, col_pos):
    cost = lax.dot_general(
        qblock, maps, (((1,), (1,)), ((), ())), preferred_element_type=jnp.float32
    )
    cost = cost * (1.0 / math.sqrt(maps.shape[1]))
    logit = conv_logits(
        cost.reshape(cost.shape[0], GRID_H, GRID_W), conv_weight, conv_bias, head_weight
    )
    heat = jax.nn.softmax(logit.reshape(cost.shape), axis=-1)
    row_est = jnp.sum(heat * row_pos, axis=-1).astype(jnp.bfloat16)
    col_est = jnp.sum(heat * col_pos, axis=-1).astype(jnp.bfloat16)
    sampled = jnp.dot(heat.astype(jnp.bfloat16), maps, preferred_element_type=jnp.float32).astype(
        jnp.bfloat16
    )
    return (sampled, row_est, col_est)


def temporal_mix(extended, temporal_taps, mix_gain, mix_out):
    mixed = (
        temporal_taps[0] * extended[:, :-2]
        + temporal_taps[1] * extended[:, 1:-1]
        + temporal_taps[2] * extended[:, 2:]
    )
    normed = mixed * lax.rsqrt(jnp.mean(mixed * mixed, axis=-1, keepdims=True) + 1e-06) * mix_gain
    hidden = jax.nn.gelu(normed).astype(jnp.bfloat16)
    rows, frames_here = (hidden.shape[0], hidden.shape[1])
    delta = jnp.dot(
        hidden.reshape(rows * frames_here, hidden.shape[2]),
        mix_out,
        preferred_element_type=jnp.float32,
    )
    return delta.reshape(rows, frames_here, 3)


def assemble(row_est, col_est, delta):
    return jnp.stack(
        [
            row_est.astype(jnp.float32) + delta[:, :, 0],
            col_est.astype(jnp.float32) + delta[:, :, 1],
            delta[:, :, 2],
        ],
        axis=1,
    )


def project(sampled, mix_in):
    rows, frames_here, chan = sampled.shape
    projected = jnp.dot(
        sampled.reshape(rows * frames_here, chan), mix_in, preferred_element_type=jnp.float32
    )
    return projected.reshape(rows, frames_here, mix_in.shape[1])


def on_device(
    feature_maps,
    query_frame,
    query_row,
    query_col,
    track_order,
    conv_weight,
    conv_bias,
    head_weight,
    mix_in,
    temporal_taps,
    mix_gain,
    mix_out,
):
    frame_count = lax.axis_size("frame")
    track_count = lax.axis_size("track")
    frame_here = lax.axis_index("frame")
    track_here = lax.axis_index("track")
    f_dev, pixels, chan = feature_maps.shape
    total = track_order.shape[0]
    tr_dev = total // track_count
    sub_rows = tr_dev // frame_count
    slots = (
        jnp.arange(frame_count, dtype=jnp.int32)[:, None] * track_count + track_here
    ) * sub_rows
    slots = (slots + jnp.arange(sub_rows, dtype=jnp.int32)[None, :]).reshape(tr_dev)
    tracks = track_order[slots]
    local_frame = query_frame[tracks] - frame_here * f_dev
    owned = (local_frame >= 0) & (local_frame < f_dev)
    pixel_ids = query_row[tracks] * GRID_W + query_col[tracks]
    flat = jnp.clip(local_frame, 0, f_dev - 1) * pixels + pixel_ids
    picks = feature_maps.reshape(f_dev * pixels, chan)[flat]
    partial_value = jnp.where(owned[:, None], picks, jnp.zeros((), picks.dtype))
    queries = lax.psum(partial_value, "frame").astype(jnp.float32).astype(jnp.bfloat16)
    positions = jnp.arange(pixels, dtype=jnp.int32)
    row_pos = (positions // GRID_W).astype(jnp.float32) / (GRID_H - 1)
    col_pos = (positions % GRID_W).astype(jnp.float32) / (GRID_W - 1)
    blk = min(tr_dev, 64)
    blocks = tr_dev // blk
    grouped = queries.reshape(blocks, blk, chan)
    sampled_list, row_list, col_list = ([], [], [])
    maps = feature_maps[0]

    def per_block(qblock):
        return block_terms(qblock, maps, conv_weight, conv_bias, head_weight, row_pos, col_pos)

    sampled_f, row_f, col_f = lax.map(per_block, grouped)
    sampled_list.append(sampled_f.reshape(tr_dev, chan))
    row_list.append(row_f.reshape(tr_dev))
    col_list.append(col_f.reshape(tr_dev))
    sampled = jnp.stack(sampled_list, axis=1)
    row_est = jnp.stack(row_list, axis=1)
    col_est = jnp.stack(col_list, axis=1)
    rims = padded_2(sampled, (("frame", 1),), 1)
    projected = project(rims, mix_in)
    global_frame = frame_here * f_dev - 1 + jnp.arange(f_dev + 2, dtype=jnp.int32)
    valid = (global_frame >= 0) & (global_frame < frame_count * f_dev)
    extended = jnp.where(valid[None, :, None], projected, 0.0)
    delta = temporal_mix(extended, temporal_taps, mix_gain, mix_out)
    local_est = assemble(row_est, col_est, delta).reshape(frame_count, sub_rows, 3, f_dev)
    gathered = lax.all_to_all(local_est, "frame", split_axis=0, concat_axis=3, tiled=True)
    return gathered.reshape(sub_rows, 3, frame_count * f_dev)


def solution(mesh):
    placed = (
        P(("clip", "frame"), None, None),
        P("clip"),
        P("clip"),
        P("clip"),
        P("clip"),
        P(),
        P(),
        P(),
        P(),
        P(),
        P(),
        P(),
    )
    return jax.shard_map(
        on_device,
        mesh=mesh,
        in_specs=placed,
        out_specs=P(("clip", "frame", "track"), None, None),
        check_vma=False,
    )
```

profile of v0, /device:TPU:0, one launch (start us, length us, event | category | flops | bytes accessed | tf_op | source)
XLA Modules:
  0.0 403.0 jit_solution(6857952410239867091)
XLA Ops:
  6.8 1.6 gather_fusion
  8.4 1.6 gather_fusion.1
  10.1 1.6 gather_fusion.2
  11.7 1.6 gather_fusion.3
  13.4 2.6 gather_fusion.4
  16.8 37.1 %all-reduce.3.cloned.1.call-done = bf16[2,64,256]{2,1,0:T(8,128)(2,1)} async-done(((bf16[2,64,256]{2,1,0:T(8,128)(2,1)}), bf16[2,64,256]{2,1,0:T(8,128)(2,1)}) %all-reduce.3.cloned.1.call-update) | async-done | bytes 65552 | tf_op jit(solution)/shard_map/psum | solution.py:126
  53.9 322.9 %while.17 = (s32[]{:T(128)}, bf16[2,64,256]{2,1,0:T(8,128)(2,1)S(1)}, bf16[2,64]{1,0:T(2,128)(2,1)S(1)}, bf16[2,64]{1,0:T(2,128)(2,1)S(1)}, f32[16]{0:T(128)S(1)...) while((s32[]{:T(128)}, ...), condition=%wide.region_6.7_spmd.clone, body=%wide.region_1.6_spmd.clone.sunk | while | flops 359751424 | bytes 14882489 | solution.py:139
  54.7 0.7 fusion.91
  55.4 0.7 fusion.92
  56.1 0.7 fusion.93
  61.1 2.4 convolution_multiply_fusion.2
  63.5 2.2 reshape.346
  65.7 142.6 %fusion.97 = (f32[64]{0:T(128)S(1)}, f32[64,64,64]{2,1,0:T(8,128)S(1)}) fusion(f32[]{:T(128)} %bitcast.408, f32[]{:T(128)} %bitcast.409, f32[]{:T(128)} %bitcast.410, f32[]{:T(128)} %bitcast.411, f32[64,64,64]{2,1,0:T(8,128)} %reshape.346, f32[]{:T(128)} %bitcast.412, f32[]{:T(128)} %bitcast.413, f32[]{:T(128)} %bitcast.414, f32[]{:T(128)} %bitcast.415, ...), kind=kLoop, calls=%fused_computation.97.clone.1 | loop fusion | flops 88080320 | bytes 2098112 | tf_op jit(solution)/shard_map/while/body/eval_jaxpr/reduce_max | solution.py:48
  208.3 1.0 fusion.98
  209.5 1.8 multiply_reduce_fusion.4
  211.3 1.6 reshape.347
  212.9 2.4 fusion.99
  215.4 0.7 fusion.90
  216.1 0.7 fusion.91
  216.9 0.7 fusion.92
  217.6 0.7 fusion.93
  222.6 2.4 convolution_multiply_fusion.2
  225.0 2.2 reshape.346
  227.2 142.6 %fusion.97 = (f32[64]{0:T(128)S(1)}, f32[64,64,64]{2,1,0:T(8,128)S(1)}) fusion(f32[]{:T(128)} %bitcast.408, f32[]{:T(128)} %bitcast.409, f32[]{:T(128)} %bitcast.410, f32[]{:T(128)} %bitcast.411, f32[64,64,64]{2,1,0:T(8,128)} %reshape.346, f32[]{:T(128)} %bitcast.412, f32[]{:T(128)} %bitcast.413, f32[]{:T(128)} %bitcast.414, f32[]{:T(128)} %bitcast.415, ...), kind=kLoop, calls=%fused_computation.97.clone.1 | loop fusion | flops 88080320 | bytes 2098112 | tf_op jit(solution)/shard_map/while/body/eval_jaxpr/reduce_max | solution.py:48
  369.7 1.0 fusion.98
  370.9 1.8 multiply_reduce_fusion.4
  372.8 1.6 reshape.347
  374.4 2.4 fusion.99
  376.8 3.3 collective-permute-start
  380.2 1.3 collective-permute-start.1
  382.1 4.3 %collective-permute-done.1 = bf16[128,1,256]{2,0,1:T(8,128)(2,1)S(1)} collective-permute-done((bf16[128,1,256]{2,0,1:T(8,128)(2,1)S(1)}, bf16[128,1,256]{2,0,1:T(8,128)(2,1)S(1)}, u32[]{:S(2)}, u32[]{:S(2)}) %collective-permute-start.1) | collective-permute-done | bytes 65568 | tf_op jit(solution)/shard_map/ppermute | solution.py:19
  387.6 7.9 %all_to_all.15 = f32[4,32,3,1]{1,3,2,0:T(1,128)S(1)} all-to-all(f32[4,32,3,1]{1,3,2,0:T(1,128)S(1)} %copy.15), channel_id=1, replica_groups=mesh['clip'=2,'frame'=4,'track'=4] {'frame'}, dimensions={0} | all-to-all | bytes 3072 | tf_op jit(solution)/shard_map/all_to_all | solution.py:153
  (71 shorter events, 13.2 us)
Async XLA Ops:
  6.5 379.8 %copy-start = (bf16[256,1024]{1,0:T(8,128)(2,1)S(1)}, bf16[256,1024]{1,0:T(8,128)(2,1)}, u32[]{:S(2)}) copy-start(bf16[256,1024]{1,0:T(8,128)(2,1)} %param.22) | copy-start | bytes 1572868
  6.5 10.2 %copy-start.4 = (f32[3,1024]{1,0:T(4,128)S(1)}, f32[3,1024]{1,0:T(4,128)}, u32[]{:S(2)}) copy-start(f32[3,1024]{1,0:T(4,128)} %param.23) | copy-start | bytes 36868
  6.5 47.4 %copy-start.1 = (f32[16,9]{1,0:T(8,128)S(1)}, f32[16,9]{1,0:T(8,128)}, u32[]{:S(2)}) copy-start(f32[16,9]{1,0:T(8,128)} %param.19) | copy-start | bytes 1732
  6.5 47.4 %copy-start.3 = (f32[16]{0:T(128)S(1)}, f32[16]{0:T(128)}, u32[]{:S(2)}) copy-start(f32[16]{0:T(128)} %param.20) | copy-start | bytes 196
  6.5 47.4 %copy-start.2 = (f32[16]{0:T(128)S(1)}, f32[16]{0:T(128)}, u32[]{:S(2)}) copy-start(f32[16]{0:T(128)} %param.21) | copy-start | bytes 196
  6.5 47.4 %all-reduce.3.cloned.1.call-start = ((), (), s32[]{:S(2)}) async-start(), calls=%async_computation.1 | async-start | bytes 131072 | tf_op jit(solution)/shard_map/psum | solution.py:126
  376.8 5.2 %collective-permute-start = (bf16[128,1,256]{2,0,1:T(8,128)(2,1)S(1)}, bf16[128,1,256]{2,0,1:T(8,128)(2,1)S(1)}, u32[]{:S(2)}, u32[]{:S(2)}) collective-permute-start(bf16[128,1,256]{2,0,1:T(8,128)(2,1)S(1)} %bitcast.589), channel_id=1, source_target_pairs={{0,4},{4,8},{8,12},{1,5},{5,9},{9,13},{2,6},{6,10},{10,14},{3,7},{... | collective-permute-start | bytes 196616 | tf_op jit(solution)/shard_map/ppermute | solution.py:16
  380.2 6.2 %collective-permute-start.1 = (bf16[128,1,256]{2,0,1:T(8,128)(2,1)S(1)}, bf16[128,1,256]{2,0,1:T(8,128)(2,1)S(1)}, u32[]{:S(2)}, u32[]{:S(2)}) collective-permute-start(bf16[128,1,256]{2,0,1:T(8,128)(2,1)S(1)} %bitcast.590), channel_id=1, source_target_pairs={{4,0},{8,4},{12,8},{5,1},{9,5},{13,9},{6,2},{10,6},{14,10},{7,3},{... | collective-permute-start | bytes 196616 | tf_op jit(solution)/shard_map/ppermute | solution.py:19
  381.7 5.3 %copy-start.5 = (bf16[1024,3]{0,1:T(4,128)(2,1)S(1)}, bf16[1024,3]{0,1:T(4,128)(2,1)}, u32[]{:S(2)}) copy-start(bf16[1024,3]{0,1:T(4,128)(2,1)} %param.25) | copy-start | bytes 18436
  381.7 5.3 %copy-start.6 = (f32[1024]{0:T(1024)S(1)}, f32[1024]{0:T(1024)}, u32[]{:S(2)}) copy-start(f32[1024]{0:T(1024)} %param.24) | copy-start | bytes 12292
Sparse Core Ops, SparseCore 0:
  16.9 37.0 all-reduce.2
where the time goes:
time: 406 us; the launch traced here: 403 us
  other arithmetic  292 us (72%)
  waiting for transfers between devices  41.8 us (10%)
  local copies, waits for them, and re-layouts  32.8 us (8%)
  between operations  13.5 us (3%)
  matrix products  10.4 us (3%)
  blocking collectives  7.93 us (2%)
  starting transfers between devices  4.66 us (1%)
    reduce_max x2, other arithmetic, block_terms(): heat = jax.nn.softmax(logit.reshape(cost.shape), axis=-1)  285 us
    psum x1, waiting for transfers between devices, on_device(): lax.psum(partial_value, 'frame').astype(jnp.float32).astype(jnp.bfloat16)  37.1 us
    slice x16, local copies, waits for them, and re-layouts, conv_logits(): conv_weight[channel, tap]  11.5 us
  transfers between devices with their start and end apart: 3, of which 3 were waited for; matrix products, arithmetic and copies ran while one was open for 0% of the time, Pallas kernels for 0%

commit v1 on v0

--- a/solution.py
+++ b/solution.py
@@ -6,6 +6,12 @@
 
 GRID_H = 64
 GRID_W = 64
+
+
+def summed_here(x, axis):
+    shards = lax.all_gather(x, axis, axis=0, tiled=False)
+    total = shards.sum(axis=0)
+    return total
 
 
 def padded_2(block, sides, width):
@@ -123,7 +129,7 @@
     flat = jnp.clip(local_frame, 0, f_dev - 1) * pixels + pixel_ids
     picks = feature_maps.reshape(f_dev * pixels, chan)[flat]
     partial_value = jnp.where(owned[:, None], picks, jnp.zeros((), picks.dtype))
-    queries = lax.psum(partial_value, "frame").astype(jnp.float32).astype(jnp.bfloat16)
+    queries = summed_here(partial_value, "frame").astype(jnp.float32).astype(jnp.bfloat16)
     positions = jnp.arange(pixels, dtype=jnp.int32)
     row_pos = (positions // GRID_W).astype(jnp.float32) / (GRID_H - 1)
     col_pos = (positions % GRID_W).astype(jnp.float32) / (GRID_W - 1)

time: 406 us -> 373 us (0.919)
  waiting for transfers between devices: 41.8 us -> 4.65 us
  blocking collectives: 7.93 us -> 24.8 us
  between operations: 13.5 us -> 0.19 us
    psum x1 -> x0, waiting for transfers between devices: 37.1 us -> none  [on_device(): lax.psum(partial_value, 'frame').astype(jnp.float32).astype(jnp.bfloat16)]
    all_gather x0 -> x1, blocking collectives: none -> 15.7 us  [summed_here(): shards = lax.all_gather(x, axis, axis=0, tiled=False)]
  transfers between devices with their start and end apart: 3 -> 2, of which waited for: 3 -> 2; matrix products, arithmetic and copies ran while one was open for 0% -> 0% of each run, Pallas kernels for 0% -> 0%
where the time goes in v1:
time: 373 us; the launch traced here: 369 us
  other arithmetic  291 us (78%)
  local copies, waits for them, and re-layouts  32.8 us (9%)
  blocking collectives  24.8 us (7%)
  matrix products  10.3 us (3%)
  starting transfers between devices  5.21 us (1%)
  waiting for transfers between devices  4.65 us (1%)
    reduce_max x2, other arithmetic, block_terms(): heat = jax.nn.softmax(logit.reshape(cost.shape), axis=-1)  285 us
    all_gather x1, blocking collectives, summed_here(): shards = lax.all_gather(x, axis, axis=0, tiled=False)  15.7 us
    slice x16, local copies, waits for them, and re-layouts, conv_logits(): conv_weight[channel, tap]  11.5 us
    all_to_all x1, blocking collectives, on_device(): lax.all_to_all(local_est, 'frame', split_axis=0, concat_axis=3, tiled=True)  9.1 us
  transfers between devices with their start and end apart: 2, of which 2 were waited for; matrix products, arithmetic and copies ran while one was open for 0% of the time, Pallas kernels for 0%

profile of v1, /device:TPU:0, one launch (start us, length us, event | category | flops | bytes accessed | tf_op | source)
XLA Modules:
  0.0 369.4 jit_solution(15781205720743745966)
XLA Ops:
  0.2 1.6 gather_fusion
  1.9 1.6 gather_fusion.1
  3.5 1.6 gather_fusion.2
  5.2 1.6 gather_fusion.3
  6.9 2.6 gather_fusion.4
  9.6 15.7 %all_gather.4 = bf16[4,128,256]{2,1,0:T(8,128)(2,1)S(1)} all-gather(bf16[1,128,256]{2,1,0:T(8,128)(2,1)S(1)} %bitcast_select_fusion), channel_id=1, replica_groups=mesh['clip'=2,'frame'=4,'track'=4] {'frame'}, dimensions={0}, use_global_device_ids=true | all-gather | bytes 327680 | tf_op jit(solution)/shard_map/all_gather | solution.py:12
  25.3 322.9 %while.17 = (s32[]{:T(128)}, bf16[2,64,256]{2,1,0:T(8,128)(2,1)S(1)}, bf16[2,64]{1,0:T(2,128)(2,1)S(1)}, bf16[2,64]{1,0:T(2,128)(2,1)S(1)}, f32[16]{0:T(128)S(1)...) while((s32[]{:T(128)}, ...), condition=%wide.region_6.7_spmd.clone, body=%wide.region_1.6_spmd.clone.sunk | while | flops 359751424 | bytes 14881981 | solution.py:145
  25.3 0.7 fusion.90
  26.1 0.7 fusion.91
  28.2 0.7 fusion.94
  29.0 0.7 fusion.95
  32.5 2.3 convolution_multiply_fusion.2
  34.9 2.2 reshape.372
  37.1 142.6 %fusion.97 = (f32[64]{0:T(128)S(1)}, f32[64,64,64]{2,1,0:T(8,128)S(1)}) fusion(f32[]{:T(128)} %bitcast.410, f32[]{:T(128)} %bitcast.411, f32[]{:T(128)} %bitcast.412, f32[]{:T(128)} %bitcast.413, f32[64,64,64]{2,1,0:T(8,128)} %reshape.372, f32[]{:T(128)} %bitcast.414, f32[]{:T(128)} %bitcast.415, f32[]{:T(128)} %bitcast.416, f32[]{:T(128)} %bitcast.417, ...), kind=kLoop, calls=%fused_computation.97.clone.1 | loop fusion | flops 88080320 | bytes 2098112 | tf_op jit(solution)/shard_map/while/body/eval_jaxpr/reduce_max | solution.py:54
  179.7 1.0 fusion.98
  180.9 1.8 multiply_reduce_fusion.4
  182.7 1.6 reshape.373
  184.4 2.4 fusion.99
  186.8 0.7 fusion.90
  187.5 0.7 fusion.91
  190.4 0.7 fusion.95
  194.0 2.3 convolution_multiply_fusion.2
  196.4 2.2 reshape.372
  198.5 142.6 %fusion.97 = (f32[64]{0:T(128)S(1)}, f32[64,64,64]{2,1,0:T(8,128)S(1)}) fusion(f32[]{:T(128)} %bitcast.410, f32[]{:T(128)} %bitcast.411, f32[]{:T(128)} %bitcast.412, f32[]{:T(128)} %bitcast.413, f32[64,64,64]{2,1,0:T(8,128)} %reshape.372, f32[]{:T(128)} %bitcast.414, f32[]{:T(128)} %bitcast.415, f32[]{:T(128)} %bitcast.416, f32[]{:T(128)} %bitcast.417, ...), kind=kLoop, calls=%fused_computation.97.clone.1 | loop fusion | flops 88080320 | bytes 2098112 | tf_op jit(solution)/shard_map/while/body/eval_jaxpr/reduce_max | solution.py:54
  341.2 1.0 fusion.98
  342.3 1.8 multiply_reduce_fusion.4
  344.2 1.6 reshape.373
  345.8 2.4 fusion.99
  348.3 3.9 %collective-permute-start = (bf16[128,1,256]{2,0,1:T(8,128)(2,1)S(1)}, bf16[128,1,256]{2,0,1:T(8,128)(2,1)S(1)}, u32[]{:S(2)}, u32[]{:S(2)}) collective-permute-start(bf16[128,1,256]{2,0,1:T(8,128)(2,1)S(1)} %bitcast.591), channel_id=1, source_target_pairs={{0,4},{4,8},{8,12},{1,5},{5,9},{9,13},{2,6},{6,10},{10,14},{3,7},{... | collective-permute-start | bytes 196616 | tf_op jit(solution)/shard_map/ppermute | solution.py:22
  352.2 1.3 collective-permute-start.1
  354.1 4.3 %collective-permute-done.1 = bf16[128,1,256]{2,0,1:T(8,128)(2,1)S(1)} collective-permute-done((bf16[128,1,256]{2,0,1:T(8,128)(2,1)S(1)}, bf16[128,1,256]{2,0,1:T(8,128)(2,1)S(1)}, u32[]{:S(2)}, u32[]{:S(2)}) %collective-permute-start.1) | collective-permute-done | bytes 65568 | tf_op jit(solution)/shard_map/ppermute | solution.py:25
  359.7 9.1 %all_to_all.15 = f32[4,32,3,1]{1,3,2,0:T(1,128)S(1)} all-to-all(f32[4,32,3,1]{1,3,2,0:T(1,128)S(1)} %copy.15), channel_id=1, replica_groups=mesh['clip'=2,'frame'=4,'track'=4] {'frame'}, dimensions={0} | all-to-all | bytes 3072 | tf_op jit(solution)/shard_map/all_to_all | solution.py:159
  (70 shorter events, 12.5 us)
Async XLA Ops:
  0.0 358.4 %copy-start = (bf16[256,1024]{1,0:T(8,128)(2,1)S(1)}, bf16[256,1024]{1,0:T(8,128)(2,1)}, u32[]{:S(2)}) copy-start(bf16[256,1024]{1,0:T(8,128)(2,1)} %param.22) | copy-start | bytes 1572868
  0.0 25.3 %copy-start.1 = (f32[16,9]{1,0:T(8,128)S(1)}, f32[16,9]{1,0:T(8,128)}, u32[]{:S(2)}) copy-start(f32[16,9]{1,0:T(8,128)} %param.19) | copy-start | bytes 1732
  0.0 25.3 %copy-start.3 = (f32[16]{0:T(128)S(1)}, f32[16]{0:T(128)}, u32[]{:S(2)}) copy-start(f32[16]{0:T(128)} %param.20) | copy-start | bytes 196
  0.0 25.3 %copy-start.2 = (f32[16]{0:T(128)S(1)}, f32[16]{0:T(128)}, u32[]{:S(2)}) copy-start(f32[16]{0:T(128)} %param.21) | copy-start | bytes 196
  25.3 328.2 %copy-start.4 = (f32[3,1024]{1,0:T(4,128)S(1)}, f32[3,1024]{1,0:T(4,128)}, u32[]{:S(2)}) copy-start(f32[3,1024]{1,0:T(4,128)} %param.23) | copy-start | bytes 36868
  348.3 5.8 %collective-permute-start = (bf16[128,1,256]{2,0,1:T(8,128)(2,1)S(1)}, bf16[128,1,256]{2,0,1:T(8,128)(2,1)S(1)}, u32[]{:S(2)}, u32[]{:S(2)}) collective-permute-start(bf16[128,1,256]{2,0,1:T(8,128)(2,1)S(1)} %bitcast.591), channel_id=1, source_target_pairs={{0,4},{4,8},{8,12},{1,5},{5,9},{9,13},{2,6},{6,10},{10,14},{3,7},{... | collective-permute-start | bytes 196616 | tf_op jit(solution)/shard_map/ppermute | solution.py:22
  352.2 6.2 %collective-permute-start.1 = (bf16[128,1,256]{2,0,1:T(8,128)(2,1)S(1)}, bf16[128,1,256]{2,0,1:T(8,128)(2,1)S(1)}, u32[]{:S(2)}, u32[]{:S(2)}) collective-permute-start(bf16[128,1,256]{2,0,1:T(8,128)(2,1)S(1)} %bitcast.592), channel_id=1, source_target_pairs={{4,0},{8,4},{12,8},{5,1},{9,5},{13,9},{6,2},{10,6},{14,10},{7,3},{... | collective-permute-start | bytes 196616 | tf_op jit(solution)/shard_map/ppermute | solution.py:25
  353.7 5.3 %copy-start.5 = (bf16[1024,3]{0,1:T(4,128)(2,1)S(1)}, bf16[1024,3]{0,1:T(4,128)(2,1)}, u32[]{:S(2)}) copy-start(bf16[1024,3]{0,1:T(4,128)(2,1)} %param.25) | copy-start | bytes 18436
  353.7 5.3 %copy-start.6 = (f32[1024]{0:T(1024)S(1)}, f32[1024]{0:T(1024)}, u32[]{:S(2)}) copy-start(f32[1024]{0:T(1024)} %param.24) | copy-start | bytes 12292
